TPU v7x, 32 devices: a whole 2x2x4 slice. The times are simulated.
32 devices in a mesh: dp: 4 (over y, core), ctx: 8 (over z, x).
Axes of the slice: x: 2, y: 2, z: 4, core: 2. Of those that a mesh axis runs over, the one named last changes fastest.
Arguments:
- hidden_in: bfloat16 [8, 1024, 768], P('dp', 'ctx'), may hold values from -6 to 6
- grad_out: bfloat16 [8, 1024, 768], P('dp', 'ctx'), may hold values from -8 to 8
- segment_ids: int32 [8, 1024], P('dp', 'ctx'), may hold values from 0 to 7, never falling along the last dimension, each value on 1 to 768 neighbouring positions
- w_qkv: float32 [768, 2304], P('dp'), may hold values from -0.21875 to 0.21875
- w_out: float32 [768, 768], P('dp'), may hold values from -1.75 to 1.75
- w_in: float32 [768, 2304], P('dp'), may hold values from -0.21875 to 0.21875
- w_down: float32 [1152, 768], P(None, 'dp'), may hold values from -0.1875 to 0.1875
- gain_attn: float32 [768], P('dp'), may hold values from 0.1 to 1.9
- gain_mlp: float32 [768], P('dp'), may hold values from 0.1 to 1.9
Outputs:
- layer_out: bfloat16 [8, 1024, 768], P('dp', 'ctx')
- grad_in: bfloat16 [8, 1024, 768], P('dp', 'ctx')
- g_w_qkv: float32 [768, 2304], P('dp')
- g_w_out: float32 [768, 768], P('dp')
- g_w_in: float32 [768, 2304], P('dp')
- g_w_down: float32 [1152, 768], P(None, 'dp')
- g_gain_attn: float32 [768], P('dp')
- g_gain_mlp: float32 [768], P('dp')
Inputs may be any that keep to these rules, and one draw needn't show every extreme that they name: `segment_ids`: ids never fall along a sequence; a document has at most (3072) // 4 tokens, and one document of each sequence has exactly that many.
All inputs are finite; a program needn't handle non-finite values.
Results may differ from a plain program's by a relative error of at most 0.018.
Values may be sent and summed in bfloat16 or wider, within the bound.
No kernel may reach another device: no remote copies, remote signals or barrier semaphores. Data moves between devices by JAX's collectives and lax.ppermute only.
A program may use at most 320 MiB of HBM per device.

v0:
```python
import math

import jax
import jax.numpy as jnp
from jax import lax
from jax.sharding import PartitionSpec as P

D = 768
HEADS = 12
HD = 64
FF = 1152


norm_eps = 1e-05
theta_base = 160000.0


def layer_norm(values, gain):
    mean_val = jnp.mean(values, axis=-1, keepdims=True)
    centred = values - mean_val
    variance = jnp.mean(centred * centred, axis=-1, keepdims=True)
    return centred * lax.rsqrt(variance + norm_eps) * gain


def rotary_tables(positions, head_size):
    half_size = head_size // 2
    exponents = jnp.arange(half_size, dtype=jnp.float32) * (2.0 / head_size)
    inv_freq = 1.0 / theta_base**exponents
    angles = positions.astype(jnp.float32)[:, None] * inv_freq[None, :]
    cosine = jnp.cos(angles)
    sine = jnp.sin(angles)
    return (jnp.concatenate([cosine, cosine], -1), jnp.concatenate([sine, sine], -1))


def rotate(values, cosine, sine):
    half_size = values.shape[-1] // 2
    turned = jnp.concatenate([-values[..., half_size:], values[..., :half_size]], -1)
    return values * cosine[:, None, :] + turned * sine[:, None, :]


def fold_blocks(carry, pieces, piece_segments, work, rows):
    count = piece_segments.shape[0]
    size = math.gcd(count, 4 * rows)
    number = count // size
    blocks = tuple((part.reshape((number, size) + part.shape[1:]) for part in pieces))
    blocks = blocks + (piece_segments.reshape(number, size),)

    def step(acc, block):
        acc = work(acc, block)
        return (acc, None)

    carry, _ = lax.scan(step, carry, blocks)
    return carry


def on_device(hidden_in, grad_out, segment_ids, w_qkv, w_out, w_in, w_down, gain_attn, gain_mlp):
    rows = hidden_in.shape[1]
    local_seqs = hidden_in.shape[0]
    score_scale = HD ** (-0.5)
    bf16 = jnp.bfloat16
    f32 = jnp.float32
    gathered = (
        lax.all_gather(w_qkv.astype(bf16), "dp", axis=0, tiled=True),
        lax.all_gather(w_out.astype(bf16), "dp", axis=0, tiled=True),
        lax.all_gather(w_in.astype(bf16), "dp", axis=0, tiled=True),
        lax.all_gather(w_down.astype(bf16), "dp", axis=1, tiled=True),
        lax.all_gather(gain_attn.astype(bf16), "dp", axis=0, tiled=True),
        lax.all_gather(gain_mlp.astype(bf16), "dp", axis=0, tiled=True),
    )
    weight_qkv, weight_out, weight_in, weight_down, gain_low_a, gain_low_b = gathered
    gain_first = gain_low_a.astype(f32)
    gain_second = gain_low_b.astype(f32)
    whole_segments = lax.all_gather(segment_ids, "ctx", axis=1, tiled=True)
    positions = lax.axis_index("ctx") * rows + jnp.arange(rows, dtype=jnp.int32)
    cosine, sine = rotary_tables(positions, HD)

    def gated(values_in):
        return jax.nn.gelu(values_in[:, :FF], approximate=False) * values_in[:, FF:]

    def turn(pair):
        return (rotate(pair[0], cosine, sine), rotate(pair[1], cosine, sine))

    def one_sequence(seq_index):
        hidden = hidden_in[seq_index].astype(f32)
        own_segments = segment_ids[seq_index]
        all_segments = whole_segments[seq_index]
        normed_first, first_back = jax.vjp(layer_norm, hidden, gain_first)
        normed_attn = normed_first.astype(bf16)
        qkv = jnp.dot(normed_attn, weight_qkv, preferred_element_type=f32)
        q_lin = qkv[:, :D].reshape(rows, HEADS, HD)
        k_lin = qkv[:, D : 2 * D].reshape(rows, HEADS, HD)
        v_lin = qkv[:, 2 * D :].reshape(rows, HEADS, HD)
        turned, turn_back = jax.vjp(turn, (q_lin, k_lin))
        queries = turned[0].astype(bf16)
        keys = turned[1].astype(bf16)
        values = v_lin.astype(bf16)

        def forward_work(acc, block):
            key_blk, value_blk, seg_blk = block
            total, summed = acc
            scores = (
                jnp.einsum("thd,shd->hts", queries, key_blk, preferred_element_type=f32)
                * score_scale
            )
            same = own_segments[:, None] == seg_blk[None, :]
            expo = jnp.where(same[None], jnp.exp(scores), 0.0)
            total = total + jnp.sum(expo, axis=-1)
            summed = summed + jnp.einsum(
                "hts,shd->thd", expo.astype(bf16), value_blk, preferred_element_type=f32
            )
            return (total, summed)

        start_fwd = (jnp.zeros((HEADS, rows), f32), jnp.zeros((rows, HEADS, HD), f32))
        key_piece = lax.all_gather(keys.reshape(rows, D), "ctx", axis=0, tiled=True)
        value_piece = lax.all_gather(values.reshape(rows, D), "ctx", axis=0, tiled=True)
        count = key_piece.shape[0]
        piece_segments = all_segments
        parts = (key_piece.reshape(count, HEADS, HD), value_piece.reshape(count, HEADS, HD))
        total, summed = fold_blocks(start_fwd, parts, piece_segments, forward_work, rows)
        total_rows = jnp.transpose(total)
        attended = (summed / total_rows[:, :, None]).reshape(rows, D).astype(bf16)
        mixed = hidden + jnp.dot(attended, weight_out, preferred_element_type=f32)
        normed_second, second_back = jax.vjp(layer_norm, mixed, gain_second)
        normed_mlp = normed_second.astype(bf16)
        gate_up = jnp.dot(normed_mlp, weight_in, preferred_element_type=f32)
        activ_f, gated_back = jax.vjp(gated, gate_up)
        activ = activ_f.astype(bf16)
        layer_out = (mixed + jnp.dot(activ, weight_down, preferred_element_type=f32)).astype(bf16)
        grad_low = grad_out[seq_index]
        g_w_down = jnp.einsum("tf,td->fd", activ, grad_low, preferred_element_type=f32)
        g_activ = jnp.einsum("td,fd->tf", grad_low, weight_down, preferred_element_type=f32)
        g_gate_up = gated_back(g_activ)[0].astype(bf16)
        g_w_in = jnp.einsum("ti,tj->ij", normed_mlp, g_gate_up, preferred_element_type=f32)
        g_normed_mlp = jnp.einsum("tj,ij->ti", g_gate_up, weight_in, preferred_element_type=f32)
        g_mixed_norm, g_gain_mlp = second_back(g_normed_mlp)
        g_mixed = grad_low.astype(f32) + g_mixed_norm
        g_mixed_low = g_mixed.astype(bf16)
        g_w_out = jnp.einsum("ti,tj->ij", attended, g_mixed_low, preferred_element_type=f32)
        g_att = jnp.einsum(
            "tj,ij->ti", g_mixed_low, weight_out, preferred_element_type=f32
        ).reshape(rows, HEADS, HD)
        g_summed = (g_att / total_rows[:, :, None]).astype(bf16)
        row_term = jnp.sum(g_att * summed, axis=-1) / (total_rows * total_rows)
        own_rows = jnp.transpose(row_term)
        all_rows = lax.all_gather(row_term, "ctx", axis=0, tiled=True)

        def query_work(acc, block):
            key_blk, value_blk, seg_blk = block
            scores = (
                jnp.einsum("thd,shd->hts", queries, key_blk, preferred_element_type=f32)
                * score_scale
            )
            same = own_segments[:, None] == seg_blk[None, :]
            expo = jnp.where(same[None], jnp.exp(scores), 0.0)
            product = jnp.einsum("thd,shd->hts", g_summed, value_blk, preferred_element_type=f32)
            g_scores = (expo * (product - own_rows[:, :, None])).astype(bf16)
            return acc + jnp.einsum("hts,shd->thd", g_scores, key_blk, preferred_element_type=f32)

        key_piece = lax.all_gather(keys.reshape(rows, D), "ctx", axis=0, tiled=True)
        value_piece = lax.all_gather(values.reshape(rows, D), "ctx", axis=0, tiled=True)
        count = key_piece.shape[0]
        piece_segments = all_segments
        parts = (key_piece.reshape(count, HEADS, HD), value_piece.reshape(count, HEADS, HD))
        g_queries = (
            fold_blocks(jnp.zeros((rows, HEADS, HD), f32), parts, piece_segments, query_work, rows)
            * score_scale
        )

        def key_work(acc, block):
            query_blk, gsum_blk, row_blk, seg_blk = block
            g_keys, g_values = acc
            scores = (
                jnp.einsum("shd,thd->hst", query_blk, keys, preferred_element_type=f32)
                * score_scale
            )
            same = seg_blk[:, None] == own_segments[None, :]
            expo = jnp.where(same[None], jnp.exp(scores), 0.0)
            g_values = g_values + jnp.einsum(
                "hst,shd->thd", expo.astype(bf16), gsum_blk, preferred_element_type=f32
            )
            product = jnp.einsum("shd,thd->hst", gsum_blk, values, preferred_element_type=f32)
            g_scores = (expo * (product - jnp.transpose(row_blk)[:, :, None])).astype(bf16)
            g_keys = g_keys + jnp.einsum(
                "hst,shd->thd", g_scores, query_blk, preferred_element_type=f32
            )
            return (g_keys, g_values)

        start_keys = (jnp.zeros((rows, HEADS, HD), f32), jnp.zeros((rows, HEADS, HD), f32))
        query_piece = lax.all_gather(queries.reshape(rows, D), "ctx", axis=0, tiled=True)
        gsum_piece = lax.all_gather(g_summed.reshape(rows, D), "ctx", axis=0, tiled=True)
        count = query_piece.shape[0]
        piece_segments = all_segments
        parts = (
            query_piece.reshape(count, HEADS, HD),
            gsum_piece.reshape(count, HEADS, HD),
            all_rows,
        )
        g_keys, g_values = fold_blocks(start_keys, parts, piece_segments, key_work, rows)
        g_keys = g_keys * score_scale
        unturned = turn_back((g_queries, g_keys))[0]
        g_qkv = jnp.concatenate(
            [unturned[0].reshape(rows, D), unturned[1].reshape(rows, D), g_values.reshape(rows, D)],
            -1,
        ).astype(bf16)
        g_w_qkv = jnp.einsum("ti,tj->ij", normed_attn, g_qkv, preferred_element_type=f32)
        g_normed_attn = jnp.einsum("tj,ij->ti", g_qkv, weight_qkv, preferred_element_type=f32)
        g_hidden_norm, g_gain_attn = first_back(g_normed_attn)
        grad_in = (g_mixed + g_hidden_norm).astype(bf16)
        terms = (g_w_qkv, g_w_out, g_w_in, g_w_down, g_gain_attn, g_gain_mlp)
        return (layer_out, grad_in, terms)

    outputs_fwd = []
    outputs_back = []
    terms = None
    for seq_index in range(local_seqs):
        layer_out, grad_in, seq_terms = one_sequence(seq_index)
        outputs_fwd.append(layer_out)
        outputs_back.append(grad_in)
        if terms is None:
            terms = seq_terms
        else:
            terms = tuple((old + new for old, new in zip(terms, seq_terms)))
    everywhere = lax.psum(terms, "ctx")
    owned = (
        lax.psum_scatter(
            everywhere[0].astype(jnp.bfloat16), "dp", scatter_dimension=0, tiled=True
        ).astype(jnp.float32),
        lax.psum_scatter(
            everywhere[1].astype(jnp.bfloat16), "dp", scatter_dimension=0, tiled=True
        ).astype(jnp.float32),
        lax.psum_scatter(
            everywhere[2].astype(jnp.bfloat16), "dp", scatter_dimension=0, tiled=True
        ).astype(jnp.float32),
        lax.psum_scatter(
            everywhere[3].astype(jnp.bfloat16), "dp", scatter_dimension=1, tiled=True
        ).astype(jnp.float32),
        lax.psum_scatter(
            everywhere[4].astype(jnp.bfloat16), "dp", scatter_dimension=0, tiled=True
        ).astype(jnp.float32),
        lax.psum_scatter(
            everywhere[5].astype(jnp.bfloat16), "dp", scatter_dimension=0, tiled=True
        ).astype(jnp.float32),
    )
    return (
        jnp.stack(outputs_fwd),
        jnp.stack(outputs_back),
        owned[0],
        owned[1],
        owned[2],
        owned[3],
        owned[4],
        owned[5],
    )


def solution(mesh):
    return jax.shard_map(
        on_device,
        mesh=mesh,
        in_specs=(
            P("dp", "ctx", None),
            P("dp", "ctx", None),
            P("dp", "ctx"),
            P("dp", None),
            P("dp", None),
            P("dp", None),
            P(None, "dp"),
            P("dp"),
            P("dp"),
        ),
        out_specs=(
            P("dp", "ctx", None),
            P("dp", "ctx", None),
            P("dp", None),
            P("dp", None),
            P("dp", None),
            P(None, "dp"),
            P("dp"),
            P("dp"),
        ),
        check_vma=False,
    )
```

profile of v0, /device:TPU:0, one launch (start us, length us, event | category | flops | bytes accessed | tf_op | source)
XLA Modules:
  0.0 1509.1 jit_solution(17270857132988866710)
XLA Ops:
  11.7 8.9 all-reduce.18
  21.1 22.6 %all-gather.13.cloned.1.call-done = bf16[768,2304]{1,0:T(8,128)(2,1)} async-done(((bf16[192,2304]{1,0:T(8,128)(2,1)}), bf16[768,2304]{1,0:T(8,128)(2,1)}) %all-gather.13.cloned.1.call-update) | async-done | bytes 3538960 | tf_op jit(solution)/shard_map/all_gather | solution.py:63
  80.0 20.6 %all_gather.55 = s32[2,1024]{1,0:T(2,128)S(1)} all-gather(s32[2,128]{1,0:T(2,128)S(1)} %copy-done.96), channel_id=1, replica_groups=mesh['dp'=4,'ctx'=8] {'ctx'}, dimensions={1}, use_global_device_ids=true | all-gather | bytes 9216 | tf_op jit(solution)/shard_map/all_gather | solution.py:73
  108.7 27.7 %all-gather.17.cloned.1.call-done = bf16[1024,768]{1,0:T(8,128)(2,1)} async-done(((bf16[128,768]{1,0:T(8,128)(2,1)}), bf16[1024,768]{1,0:T(8,128)(2,1)}) %all-gather.17.cloned.1.call-update) | async-done | bytes 1572880 | tf_op jit(solution)/shard_map/all_gather | solution.py:115
  142.3 39.3 %all-gather.25.cloned.1.call-done = bf16[1024,768]{1,0:T(8,128)(2,1)} async-done(((bf16[128,768]{1,0:T(8,128)(2,1)}), bf16[1024,768]{1,0:T(8,128)(2,1)}) %all-gather.25.cloned.1.call-update) | async-done | bytes 1572880 | tf_op jit(solution)/shard_map/all_gather | solution.py:114
  187.4 10.3 while.75
  197.7 28.9 %all-gather.15.cloned.1.call-done = bf16[1024,768]{1,0:T(8,128)(2,1)} async-done(((bf16[128,768]{1,0:T(8,128)(2,1)}), bf16[1024,768]{1,0:T(8,128)(2,1)}) %all-gather.15.cloned.1.call-update) | async-done | bytes 1572880 | tf_op jit(solution)/shard_map/all_gather | solution.py:114
  229.2 3.9 reshape_reshape.28
  234.9 10.7 while.74
  250.6 27.2 %all-gather.21.cloned.1.call-done = bf16[768,2304]{1,0:T(8,128)(2,1)} async-done(((bf16[192,2304]{1,0:T(8,128)(2,1)}), bf16[768,2304]{1,0:T(8,128)(2,1)}) %all-gather.21.cloned.1.call-update) | async-done | bytes 3538960 | tf_op jit(solution)/shard_map/all_gather | solution.py:65
  280.6 20.2 %all-gather.23.cloned.1.call-done = bf16[1152,768]{0,1:T(8,128)(2,1)} async-done(((bf16[1152,192]{0,1:T(8,128)(2,1)}), bf16[1152,768]{0,1:T(8,128)(2,1)}) %all-gather.23.cloned.1.call-update) | async-done | bytes 1769488 | tf_op jit(solution)/shard_map/all_gather | solution.py:66
  329.6 4.5 convolution_add_fusion.2
  334.7 12.3 all-gather.33.cloned.1.call-done
  351.5 40.5 %all-gather.29.cloned.1.call-done = bf16[1024,768]{1,0:T(8,128)(2,1)} async-done(((bf16[128,768]{1,0:T(8,128)(2,1)}), bf16[1024,768]{1,0:T(8,128)(2,1)}) %all-gather.29.cloned.1.call-update) | async-done | bytes 1572880 | tf_op jit(solution)/shard_map/all_gather | solution.py:189
  397.2 30.7 %all_gather.71 = f32[1024,12]{0,1:T(8,128)S(1)} all-gather(f32[128,12]{0,1:T(8,128)S(1)} %copy-done.70), channel_id=1, replica_groups=mesh['dp'=4,'ctx'=8] {'ctx'}, dimensions={0}, use_global_device_ids=true | all-gather | bytes 55296 | tf_op jit(solution)/shard_map/all_gather | solution.py:145
  428.6 30.5 %all_gather.68 = f32[1024,12]{0,1:T(8,128)S(1)} all-gather(f32[128,12]{0,1:T(8,128)S(1)} %copy-done.71), channel_id=1, replica_groups=mesh['dp'=4,'ctx'=8] {'ctx'}, dimensions={0}, use_global_device_ids=true | all-gather | bytes 55296 | tf_op jit(solution)/shard_map/all_gather | solution.py:145
  460.4 4.1 fusion.208
  464.4 13.7 while.78
  478.3 7.6 convolution_add_fusion
  486.5 14.0 while.76
  504.8 16.5 %all-gather.31.cloned.1.call-done = bf16[1024,768]{1,0:T(8,128)(2,1)} async-done(((bf16[128,768]{1,0:T(8,128)(2,1)}), bf16[1024,768]{1,0:T(8,128)(2,1)}) %all-gather.31.cloned.1.call-update) | async-done | bytes 1572880 | tf_op jit(solution)/shard_map/all_gather | solution.py:190
  525.7 22.4 %while.79 = (s32[]{:T(128)}, f32[128,12,64]{0,2,1:T(8,128)}, f32[128,12,64]{0,2,1:T(8,128)}, bf16[2,512,12,64]{1,3,2,0:T(8,128)(2,1)}, s32[2,512]{1,0:T(2,128)S(...) while((s32[]{:T(128)}, f32[128,12,64]{0,2,1:T(8,128)}, ...), condition=%wide.region_29.30_spmd.clone, body=%wide.region_28.29_spmd.clone.sunk | while | flops 409403392 | bytes 14885015 | solution.py:52
  541.5 3.9 fusion.372
  549.8 22.5 %while.77 = (s32[]{:T(128)}, f32[128,12,64]{0,2,1:T(8,128)}, f32[128,12,64]{0,2,1:T(8,128)}, bf16[2,512,12,64]{1,3,2,0:T(8,128)(2,1)}, s32[2,512]{1,0:T(2,128)S(...) while((s32[]{:T(128)}, f32[128,12,64]{0,2,1:T(8,128)}, ...), condition=%wide.region_20.21_spmd.clone, body=%wide.region_19.20_spmd.clone.sunk | while | flops 409403392 | bytes 14885015 | solution.py:52
  565.5 3.9 fusion.355
  583.2 4.1 convolution_add_fusion.1
  587.4 769.6 %all-reduce.20 = (bf16[768,2304]{1,0:T(8,128)(2,1)}, bf16[768,768]{1,0:T(8,128)(2,1)}, bf16[768,2304]{1,0:T(8,128)(2,1)}, bf16[1152,768]{0,1:T(8,128)(2,1)}, bf1...) all-reduce(f32[768,2304]{1,0:T(8,128)} %convolution_add_fusion.1, ...), channel_id=1, replica_groups=mesh['dp'=4,'ctx'=8] {'ctx'}, use_global_device_ids=true, to_apply=%region_32.33 | all-reduce | flops 5015040 | bytes 30090240 | tf_op jit(solution)/shard_map/psum | solution.py:223
  1363.0 7.0 all-reduce.17
  1375.1 6.2 reduce-scatter.7.cloned.1.call-done
  1383.1 30.8 %reduce-scatter.11.cloned.1.call-done = bf16[1152,192]{0,1:T(8,128)(2,1)} async-done(((bf16[1152,768]{0,1:T(8,128)(2,1)}), bf16[1152,192]{0,1:T(8,128)(2,1)}) %reduce-scatter.11.cloned.1.call-update) | async-done | bytes 442384 | tf_op jit(solution)/shard_map/reduce_scatter | solution.py:234
  1415.9 40.9 %reduce-scatter.9.cloned.1.call-done = bf16[192,2304]{1,0:T(8,128)(2,1)} async-done(((bf16[768,2304]{1,0:T(8,128)(2,1)}), bf16[192,2304]{1,0:T(8,128)(2,1)}) %reduce-scatter.9.cloned.1.call-update) | async-done | bytes 884752 | tf_op jit(solution)/shard_map/reduce_scatter | solution.py:231
  1459.3 40.6 %reduce-scatter.5.cloned.1.call-done = bf16[192,2304]{1,0:T(8,128)(2,1)} async-done(((bf16[768,2304]{1,0:T(8,128)(2,1)}), bf16[192,2304]{1,0:T(8,128)(2,1)}) %reduce-scatter.5.cloned.1.call-update) | async-done | bytes 884752 | tf_op jit(solution)/shard_map/reduce_scatter | solution.py:225
  (481 shorter events, 237.3 us)
Async XLA Ops:
  7.2 36.5 %all-gather.13.cloned.1.call-start = ((), (), s32[]{:S(2)}) async-start(), calls=%async_computation.4 | async-start | bytes 4423680 | tf_op jit(solution)/shard_map/all_gather | solution.py:63
  9.8 94.6 %all-gather.27.cloned.1.call-start = ((), (), s32[]{:S(2)}) async-start(), calls=%async_computation.11 | async-start | bytes 1769472 | tf_op jit(solution)/shard_map/all_gather | solution.py:115
  47.1 89.4 %all-gather.17.cloned.1.call-start = ((), (), s32[]{:S(2)}) async-start(), calls=%async_computation.6 | async-start | bytes 1769472 | tf_op jit(solution)/shard_map/all_gather | solution.py:115
  50.6 130.9 %all-gather.25.cloned.1.call-start = ((), (), s32[]{:S(2)}) async-start(), calls=%async_computation.10 | async-start | bytes 1769472 | tf_op jit(solution)/shard_map/all_gather | solution.py:114
  72.5 154.2 %all-gather.15.cloned.1.call-start = ((), (), s32[]{:S(2)}) async-start(), calls=%async_computation.5 | async-start | bytes 1769472 | tf_op jit(solution)/shard_map/all_gather | solution.py:114
  73.0 174.6 %all-gather.19.cloned.1.call-start = ((), (), s32[]{:S(2)}) async-start(), calls=%async_computation.7 | async-start | bytes 1474560 | tf_op jit(solution)/shard_map/all_gather | solution.py:64
  75.0 202.9 %all-gather.21.cloned.1.call-start = ((), (), s32[]{:S(2)}) async-start(), calls=%async_computation.8 | async-start | bytes 4423680 | tf_op jit(solution)/shard_map/all_gather | solution.py:65
  77.6 223.2 %all-gather.23.cloned.1.call-start = ((), (), s32[]{:S(2)}) async-start(), calls=%async_computation.9 | async-start | bytes 2211840 | tf_op jit(solution)/shard_map/all_gather | solution.py:66
  78.5 268.5 %all-gather.33.cloned.1.call-start = ((), (), s32[]{:S(2)}) async-start(), calls=%async_computation.14 | async-start | bytes 1769472 | tf_op jit(solution)/shard_map/all_gather | solution.py:189
  79.2 312.9 %all-gather.29.cloned.1.call-start = ((), (), s32[]{:S(2)}) async-start(), calls=%async_computation.12 | async-start | bytes 1769472 | tf_op jit(solution)/shard_map/all_gather | solution.py:189
  104.0 396.5 %all-gather.35.cloned.1.call-start = ((), (), s32[]{:S(2)}) async-start(), calls=%async_computation.15 | async-start | bytes 1769472 | tf_op jit(solution)/shard_map/all_gather | solution.py:190
  197.7 31.5 %copy-start.4 = (bf16[2,512,12,64]{1,3,2,0:T(8,128)(2,1)}, bf16[2,512,12,64]{1,3,2,0:T(8,128)(2,1)S(1)}, u32[]{:S(2)}) copy-start(bf16[2,512,12,64]{1,3,2,0:T(8,128)(2,1)S(1)} %get-tuple-element.1436) | copy-start | bytes 4718596
  249.6 63.1 %copy-start.5 = (f32[128,768]{1,0:T(8,128)}, f32[128,768]{1,0:T(8,128)S(1)}, u32[]{:S(2)}) copy-start(f32[128,768]{1,0:T(8,128)S(1)} %get-tuple-element.869) | copy-start | bytes 1179652
  249.6 28.3 %copy-start.55 = (f32[768]{0:T(1024)S(1)}, f32[768]{0:T(1024)}, u32[]{:S(2)}) copy-start(f32[768]{0:T(1024)} %convert_element_type.229) | copy-start | bytes 9220
  249.6 30.9 %copy-start.79 = (f32[128]{0:T(128)}, f32[128]{0:T(128)S(1)}, u32[]{:S(2)}) copy-start(f32[128]{0:T(128)S(1)} %broadcast_multiply_fusion.6) | copy-start | bytes 1540
  249.8 30.7 %copy-start.104 = (f32[128]{0:T(128)}, f32[128]{0:T(128)S(1)}, u32[]{:S(2)}) copy-start(f32[128]{0:T(128)S(1)} %multiply_reduce_fusion.6) | copy-start | bytes 1540
  249.8 30.7 %copy-start.89 = (f32[128]{0:T(128)}, f32[128]{0:T(128)S(1)}, u32[]{:S(2)}) copy-start(f32[128]{0:T(128)S(1)} %fusion.214) | copy-start | bytes 1540
  250.4 62.3 %copy-start.74 = (f32[128]{0:T(128)}, f32[128]{0:T(128)S(1)}, u32[]{:S(2)}) copy-start(f32[128]{0:T(128)S(1)} %broadcast_multiply_fusion.8) | copy-start | bytes 1540
  250.6 62.1 %copy-start.87 = (f32[128]{0:T(128)}, f32[128]{0:T(128)S(1)}, u32[]{:S(2)}) copy-start(f32[128]{0:T(128)S(1)} %fusion.212) | copy-start | bytes 1540
  250.6 50.2 %copy-start.31 = (bf16[2,128,768]{2,1,0:T(8,128)(2,1)S(1)}, bf16[2,128,768]{2,1,0:T(8,128)(2,1)}, u32[]{:S(2)}) copy-start(bf16[2,128,768]{2,1,0:T(8,128)(2,1)} %param.22) | copy-start | bytes 1179652
  329.5 191.8 %all-gather.31.cloned.1.call-start = ((), (), s32[]{:S(2)}) async-start(), calls=%async_computation.13 | async-start | bytes 1769472 | tf_op jit(solution)/shard_map/all_gather | solution.py:190
  395.0 33.6 %copy-start.71 = (f32[128,12]{0,1:T(8,128)S(1)}, f32[128,12]{0,1:T(8,128)}, u32[]{:S(2)}) copy-start(f32[128,12]{0,1:T(8,128)} %multiply_divide_fusion.1) | copy-start | bytes 18436
  395.0 64.7 %copy-start.69 = (f32[128,12]{0,1:T(8,128)S(1)}, f32[128,12]{0,1:T(8,128)}, u32[]{:S(2)}) copy-start(f32[128,12]{0,1:T(8,128)} %copy-done.68) | copy-start | bytes 18436
  395.0 65.3 %copy-start.22 = (f32[128,1152]{1,0:T(8,128)S(1)}, f32[128,1152]{1,0:T(8,128)}, u32[]{:S(2)}) copy-start(f32[128,1152]{1,0:T(8,128)} %copy-done.21) | copy-start | bytes 1769476
  395.0 65.3 %copy-start.38 = (f32[128,1152]{1,0:T(8,128)S(1)}, f32[128,1152]{1,0:T(8,128)}, u32[]{:S(2)}) copy-start(f32[128,1152]{1,0:T(8,128)} %copy-done.37) | copy-start | bytes 1769476
  395.1 65.3 %copy-start.57 = (f32[768]{0:T(1024)S(1)}, f32[768]{0:T(1024)}, u32[]{:S(2)}) copy-start(f32[768]{0:T(1024)} %convert_element_type.229) | copy-start | bytes 9220
  395.1 65.3 %copy-start.75 = (f32[128]{0:T(128)S(1)}, f32[128]{0:T(128)}, u32[]{:S(2)}) copy-start(f32[128]{0:T(128)} %copy-done.74) | copy-start | bytes 1540
  395.1 65.3 %copy-start.88 = (f32[128]{0:T(128)S(1)}, f32[128]{0:T(128)}, u32[]{:S(2)}) copy-start(f32[128]{0:T(128)} %copy-done.87) | copy-start | bytes 1540
  478.2 903.1 %reduce-scatter.7.cloned.1.call-start = ((), (), s32[]{:S(2)}) async-start(), calls=%async_computation.17 | async-start | bytes 1474560 | tf_op jit(solution)/shard_map/reduce_scatter | solution.py:228
  1357.0 56.9 %reduce-scatter.11.cloned.1.call-start = ((), (), s32[]{:S(2)}) async-start(), calls=%async_computation.19 | async-start | bytes 2211840 | tf_op jit(solution)/shard_map/reduce_scatter | solution.py:234
  1357.6 99.2 %reduce-scatter.9.cloned.1.call-start = ((), (), s32[]{:S(2)}) async-start(), calls=%async_computation.18 | async-start | bytes 4423680 | tf_op jit(solution)/shard_map/reduce_scatter | solution.py:231
  1358.2 141.7 %reduce-scatter.5.cloned.1.call-start = ((), (), s32[]{:S(2)}) async-start(), calls=%async_computation.16 | async-start | bytes 4423680 | tf_op jit(solution)/shard_map/reduce_scatter | solution.py:225
  (98 other events, 476.3 us)
Sparse Core Ops, SparseCore 0:
  10.2 33.4 all-gather.12
  47.2 44.1 all-gather.26
  93.6 42.8 all-gather.16
  138.5 42.9 all-gather.24
  183.6 42.9 all-gather.14
  228.6 16.2 all-gather.18
  247.0 30.7 all-gather.20
  280.0 20.7 all-gather.22
  303.0 44.0 all-gather.32
  349.0 42.9 all-gather.28
  394.3 43.7 all-gather.34
  478.3 43.0 all-gather.30
  1357.1 24.1 reduce-scatter.6
  1384.5 29.3 reduce-scatter.10
  1416.3 40.4 reduce-scatter.8
  1459.4 40.4 reduce-scatter.4
where the time goes:
time: 1520 us; the launch traced here: 1510 us
  blocking collectives  867 us (57%)
  waiting for transfers between devices  357 us (23%)
  matrix products  121 us (8%)
  local copies, waits for them, and re-layouts  84.4 us (6%)
  other arithmetic  59.8 us (4%)
  between operations  17.4 us (1%)
    psum x1, blocking collectives, on_device(): everywhere = lax.psum(terms, 'ctx')  770 us
    all_gather x2, waiting for transfers between devices, one_sequence(): key_piece = lax.all_gather(keys.reshape(rows, D), 'ctx', axis=0, tiled=True)  68.2 us
    all_gather x2, blocking collectives, one_sequence(): all_rows = lax.all_gather(row_term, 'ctx', axis=0, tiled=True)  61.2 us
    all_gather x2, waiting for transfers between devices, one_sequence(): lax.all_gather(queries.reshape(rows, D), 'ctx', axis=0, tiled=True)  52.8 us
    reduce_scatter x1, waiting for transfers between devices, on_device(): lax.psum_scatter(everywhere[2].astype(jnp.bfloat16), 'dp', scatter_dimens...  40.9 us
    reduce_scatter x1, waiting for transfers between devices, on_device(): lax.psum_scatter(everywhere[0].astype(jnp.bfloat16), 'dp', scatter_dimens...  40.6 us
    reduce_scatter x1, waiting for transfers between devices, on_device(): lax.psum_scatter(everywhere[3].astype(jnp.bfloat16), 'dp', scatter_dimens...  30.8 us
  transfers between devices with their start and end apart: 16, of which 13 were waited for; matrix products, arithmetic and copies ran while one was open for 12% of the time, Pallas kernels for 0%

commit v1 on v0

--- a/solution.py
+++ b/solution.py
@@ -3,6 +3,8 @@
 import jax
 import jax.numpy as jnp
 from jax import lax
+from jax.experimental import pallas as pl
+from jax.experimental.pallas import tpu as pltpu
 from jax.sharding import PartitionSpec as P
 
 D = 768
@@ -253,9 +255,292 @@
     )
 
 
+HALF = 384
+PIECE = 24
+
+
+def send(values, mask):
+    return lax.ppermute(values, ("dp", "ctx"), [(i, i ^ mask) for i in range(32)])
+
+
+def send_swapped(values, mask):
+    def target(i):
+        core, high = (i >> 3) & 1, (i >> 2) & 1
+        return (i & ~12) | (high << 3) | (core << 2)
+
+    return lax.ppermute(values, ("dp", "ctx"), [(i, target(i) ^ mask) for i in range(32)])
+
+
+def pick(flag, first, second):
+    return jnp.where(flag == 0, first, second)
+
+
+def pieces_kernel(order, me_ref, source_ref, out_ref):
+    me = me_ref[0]
+    for slot, mask in enumerate(order):
+        start = pl.multiple_of((me ^ mask) * PIECE, 8)
+        out_ref[slot] = source_ref[pl.ds(start, PIECE), :].astype(out_ref.dtype)
+
+
+def natural_kernel(order, me_ref, source_ref, out_ref):
+    me = me_ref[0]
+    for slot, mask in enumerate(order):
+        start = pl.multiple_of((me ^ mask) * PIECE, 8)
+        out_ref[pl.ds(start, PIECE), :] = source_ref[slot].astype(out_ref.dtype)
+
+
+VM = pl.BlockSpec(memory_space=pltpu.VMEM)
+SM = pl.BlockSpec(memory_space=pltpu.SMEM)
+
+
+def to_pieces(values, me, order):
+    return pl.pallas_call(
+        lambda *refs: pieces_kernel(order, *refs),
+        out_shape=jax.ShapeDtypeStruct((len(order), PIECE, values.shape[1]), jnp.bfloat16),
+        in_specs=[SM, VM],
+        out_specs=VM,
+        compiler_params=pltpu.CompilerParams(vmem_limit_bytes=48 << 20),
+    )(me, values)
+
+
+def to_natural(pieces, me, order, kind):
+    return pl.pallas_call(
+        lambda *refs: natural_kernel(order, *refs),
+        out_shape=jax.ShapeDtypeStruct((len(order) * PIECE, pieces.shape[2]), kind),
+        in_specs=[SM, VM],
+        out_specs=VM,
+        compiler_params=pltpu.CompilerParams(vmem_limit_bytes=48 << 20),
+    )(me, pieces)
+
+
+def plus(first, second):
+    return (first.astype(jnp.float32) + second.astype(jnp.float32)).astype(jnp.bfloat16)
+
+
+XZ = [(dx) | (dz << 1) for dx in range(2) for dz in range(4)]
+
+
+def reduce_xz(part):
+    part = part.reshape((2, 4) + part.shape[1:])
+    part = plus(part[0], send(part[1], 1))
+    total = part[0].astype(jnp.float32)
+    for dz in range(1, 4):
+        total = total + send(part[dz], 2 * dz).astype(jnp.float32)
+    total = total.astype(jnp.bfloat16)
+    near = jnp.stack([total] + [send(total, 2 * dz) for dz in range(1, 4)])
+    far = send(near, 1)
+    return jnp.concatenate([near, far])
+
+
+def rows_of(shards, dp):
+    count = shards[0].shape[0]
+    whole = jnp.zeros((4 * count,) + shards[0].shape[1:], shards[0].dtype)
+    for mask, shard in zip((0, 1, 2, 3), shards):
+        whole = lax.dynamic_update_slice(
+            whole, shard, ((dp ^ mask) * count,) + (0,) * (shard.ndim - 1)
+        )
+    return whole
+
+
+def gather_dp(shard, dp):
+    return rows_of([shard, send(shard, 8), send(shard, 16), send(shard, 24)], dp)
+
+
+def norm_parts(values):
+    mean_val = jnp.mean(values, axis=-1, keepdims=True)
+    centred = values - mean_val
+    variance = jnp.mean(centred * centred, axis=-1, keepdims=True)
+    scale = lax.rsqrt(variance + norm_eps)
+    return centred * scale, scale
+
+
+def norm_back(xhat, scale, grad, gain):
+    e = grad * gain
+    return scale * (
+        e
+        - jnp.mean(e, axis=-1, keepdims=True)
+        - xhat * jnp.mean(e * xhat, axis=-1, keepdims=True)
+    )
+
+
+def paired_chips(hidden_in, grad_out, segment_ids, w_qkv, w_out, w_in, w_down, gain_attn, gain_mlp):
+    bf16, f32 = jnp.bfloat16, jnp.float32
+    dp, ctx = lax.axis_index("dp"), lax.axis_index("ctx")
+    me = dp * 8 + ctx
+    me_ref = me.reshape(1).astype(jnp.int32)
+    y, c = dp // 2, dp % 2
+    zl, x = (ctx // 2) % 2, ctx % 2
+    rows = hidden_in.shape[1]
+    own = 2 * rows
+    score_scale = HD ** (-0.5)
+
+    def my_columns(core):
+        return jnp.concatenate(
+            [lax.dynamic_slice_in_dim(w_qkv, t * D + core * HALF, HALF, 1) for t in range(3)], 1
+        ).astype(bf16)
+
+    mine, other = my_columns(c), my_columns(1 - c)
+    weight_qkv = rows_of([mine, send(other, 8), send(mine, 16), send(other, 24)], dp)
+    gains = jnp.stack([gain_attn, gain_mlp]).astype(bf16).reshape(1, 2, 192)
+    gains = gather_dp(gains, dp).transpose(1, 0, 2).reshape(2, D).astype(f32)
+    gain_first, gain_second = gains[0], gains[1]
+
+    def to_chips(values):
+        return (
+            send_swapped(pick(zl, values[0], values[1]), 0),
+            send_swapped(pick(zl, values[1], values[0]), 2),
+        )
+
+    def from_chips(values):
+        block_a, block_b = send_swapped(values[:rows], 0), send_swapped(values[rows:], 2)
+        return jnp.stack([pick(zl, block_a, block_b), pick(zl, block_b, block_a)])
+
+    def spread(values):
+        peer = send(values, 8)
+        across = send(values, 1)
+        return jnp.concatenate([values, peer, across, send(across, 8)])
+
+    hidden_own = jnp.concatenate(to_chips(hidden_in))
+    segs_own = jnp.concatenate(to_chips(segment_ids))
+    grad_low = jnp.concatenate(to_chips(grad_out))
+    hidden = spread(hidden_own)
+    segs = spread(segs_own)
+    within = jnp.arange(rows, dtype=jnp.int32)
+    starts = []
+    for far in range(2):
+        for core in range(2):
+            for low in range(2):
+                starts.append((2 * (2 * (c ^ core) + (zl ^ low)) + (x ^ far)) * rows + within)
+    cosine, sine = rotary_tables(jnp.concatenate(starts), HD)
+    count = 4 * own
+    near = 2 * own
+
+    xhat, scale = norm_parts(hidden.astype(f32))
+    normed = (xhat * gain_first).astype(bf16)
+    q_lin = jnp.dot(normed[:near], weight_qkv[:, :HALF], preferred_element_type=f32)
+    kv_lin = jnp.dot(normed, weight_qkv[:, HALF:], preferred_element_type=f32)
+    heads = HEADS // 2
+    queries = rotate(q_lin.reshape(near, heads, HD), cosine[:near], sine[:near]).astype(bf16)
+    keys = rotate(kv_lin[:, :HALF].reshape(count, heads, HD), cosine, sine).astype(bf16)
+    values = kv_lin[:, HALF:].reshape(count, heads, HD).astype(bf16)
+    scores = jnp.einsum("thd,shd->hts", queries, keys, preferred_element_type=f32) * score_scale
+    same = segs[:near, None] == segs[None, :]
+    expo = jnp.where(same[None], jnp.exp(scores), 0.0)
+    total = jnp.sum(expo, axis=-1).T[:, :, None]
+    probs = expo.astype(bf16)
+    summed = jnp.einsum("hts,shd->thd", probs, values, preferred_element_type=f32)
+    attended = (summed / total).reshape(near, HALF).astype(bf16)
+    attended = jnp.concatenate([attended[:own], send(attended[own:], 8)], 1)
+
+    weight_out = gather_dp(w_out.astype(bf16), dp)
+    weight_out = jnp.concatenate(
+        [
+            lax.dynamic_slice_in_dim(weight_out, c * HALF, HALF, 0),
+            lax.dynamic_slice_in_dim(weight_out, (1 - c) * HALF, HALF, 0),
+        ]
+    )
+    weight_in = gather_dp(w_in.astype(bf16), dp)
+    weight_down = gather_dp(w_down.T.astype(bf16), dp)
+
+    mixed = hidden_own.astype(f32) + jnp.dot(attended, weight_out, preferred_element_type=f32)
+    xhat_mlp, scale_mlp = norm_parts(mixed)
+    normed_mlp = (xhat_mlp * gain_second).astype(bf16)
+    gate_up = jnp.dot(normed_mlp, weight_in, preferred_element_type=f32)
+    gate, upper = gate_up[:, :FF], gate_up[:, FF:]
+    chance = 0.5 * (1.0 + lax.erf(gate * math.sqrt(0.5)))
+    bell = jnp.exp(-0.5 * gate * gate) * (1.0 / math.sqrt(2.0 * math.pi))
+    activ = (gate * chance * upper).astype(bf16)
+    down = jnp.einsum("tf,df->td", activ, weight_down, preferred_element_type=f32)
+    layer_out = from_chips((mixed + down).astype(bf16))
+    g_activ = jnp.dot(grad_low, weight_down, preferred_element_type=f32)
+    g_gate_up = jnp.concatenate(
+        [g_activ * upper * (chance + gate * bell), g_activ * gate * chance], 1
+    ).astype(bf16)
+    g_w_down = jnp.einsum("td,tf->df", grad_low, activ, preferred_element_type=f32)
+    g_w_in = jnp.einsum("ti,tj->ij", normed_mlp, g_gate_up, preferred_element_type=f32)
+    g_normed_mlp = jnp.einsum("tj,ij->ti", g_gate_up, weight_in, preferred_element_type=f32)
+    g_mixed = grad_low.astype(f32) + norm_back(xhat_mlp, scale_mlp, g_normed_mlp, gain_second)
+    g_gain_mlp = jnp.sum(xhat_mlp * g_normed_mlp, axis=0)
+    g_mixed_low = g_mixed.astype(bf16)
+    g_w_out = jnp.einsum("ti,tj->ij", attended, g_mixed_low, preferred_element_type=f32)
+    g_att = jnp.einsum("tj,ij->ti", g_mixed_low, weight_out, preferred_element_type=f32)
+
+    g_att = g_att.astype(bf16)
+    g_att = jnp.concatenate([g_att[:, :HALF], send(g_att[:, HALF:], 8)]).astype(f32)
+    g_att = g_att.reshape(near, heads, HD)
+    g_summed = (g_att / total).astype(bf16)
+    row_term = (jnp.sum(g_att * summed, axis=-1, keepdims=True) / (total * total))[:, :, 0].T
+    product = jnp.einsum("thd,shd->hts", g_summed, values, preferred_element_type=f32)
+    g_scores = (probs.astype(f32) * (product - row_term[:, :, None])).astype(bf16)
+    g_queries = jnp.einsum("hts,shd->thd", g_scores, keys, preferred_element_type=f32)
+    g_keys = jnp.einsum("hts,thd->shd", g_scores, queries, preferred_element_type=f32)
+    g_values = jnp.einsum("hts,thd->shd", probs, g_summed, preferred_element_type=f32)
+
+    def turn_back(grad, cos, sin):
+        turned = grad * sin[:, None, :]
+        turned = jnp.concatenate([turned[..., HD // 2 :], -turned[..., : HD // 2]], -1)
+        return grad * cos[:, None, :] + turned
+
+    g_q = turn_back(g_queries * score_scale, cosine[:near], sine[:near])
+    g_q = g_q.reshape(near, HALF).astype(bf16)
+    g_k = turn_back(g_keys * score_scale, cosine, sine).reshape(count, HALF)
+    g_kv = jnp.concatenate([g_k, g_values.reshape(count, HALF)], 1).astype(bf16)
+    g_w_qkv = jnp.concatenate(
+        [
+            jnp.einsum("ti,tj->ij", normed[:near], g_q, preferred_element_type=f32),
+            jnp.einsum("ti,tj->ij", normed, g_kv, preferred_element_type=f32),
+        ],
+        1,
+    )
+    g_near = jnp.einsum("tj,ij->ti", g_q, weight_qkv[:, :HALF], preferred_element_type=f32)
+    g_normed = jnp.einsum("tj,ij->ti", g_kv, weight_qkv[:, HALF:], preferred_element_type=f32)
+    g_normed = g_normed + jnp.pad(g_near, ((0, near), (0, 0)))
+    g_gain_attn = jnp.sum(xhat * g_normed, axis=0)
+    g_normed = g_normed.astype(bf16).reshape(2, 2, own, D)
+    g_normed = plus(g_normed[:, 0], send(g_normed[:, 1], 8))
+    g_normed = g_normed[0].astype(f32) + send(g_normed[1], 1).astype(f32)
+    grad_in = g_mixed + norm_back(xhat[:own], scale[:own], g_normed, gain_first)
+    grad_in = from_chips(grad_in.astype(bf16))
+
+    all_masks = [(dc << 3) | (dy << 4) | m for dc in range(2) for dy in range(2) for m in XZ]
+
+    def reduce_all(grad):
+        part = to_pieces(grad, me_ref, all_masks).reshape(2, 2, 8, PIECE, grad.shape[1])
+        part = plus(part[0], send(part[1], 8))
+        part = plus(part[0], send(part[1], 16))
+        return to_natural(reduce_xz(part), me_ref % 8, XZ, f32)
+
+    g_w_out = jnp.concatenate(
+        [
+            lax.dynamic_slice_in_dim(g_w_out, c * HALF, HALF, 0),
+            lax.dynamic_slice_in_dim(g_w_out, (1 - c) * HALF, HALF, 0),
+        ]
+    )
+    g_w_down, g_w_in, g_w_out = reduce_all(g_w_down), reduce_all(g_w_in), reduce_all(g_w_out)
+
+    core_last = [(dy << 4) | (dc << 3) | m for dy in range(2) for dc in range(2) for m in XZ]
+    part = to_pieces(g_w_qkv, me_ref, core_last).reshape(2, 16, PIECE, 3 * HALF)
+    part = plus(part[0], send(part[1], 16)).reshape(2, 8, PIECE, 3 * HALF)
+    part = jnp.stack([reduce_xz(part[0]), reduce_xz(part[1])])
+    other_half = send(part[1], 8)
+    mine = to_natural(part[0], me_ref % 8, XZ, f32)
+    other = to_natural(other_half, me_ref % 8, XZ, f32)
+    low, high = pick(c, mine, other), pick(c, other, mine)
+    g_w_qkv = jnp.concatenate(
+        [h[:, t * HALF : (t + 1) * HALF] for t in range(3) for h in (low, high)], 1
+    )
+
+    g_gains = jnp.stack([g_gain_attn, g_gain_mlp])
+    for mask in (8, 16, 1, 2, 4):
+        g_gains = g_gains + send(g_gains, mask)
+    g_gains = lax.dynamic_slice_in_dim(g_gains, dp * 192, 192, 1)
+    return (layer_out, grad_in, g_w_qkv, g_w_out, g_w_in, g_w_down.T, g_gains[0], g_gains[1])
+
+
 def solution(mesh):
+    whole_fit = mesh.shape["dp"] == 4 and mesh.shape["ctx"] == 8
     return jax.shard_map(
-        on_device,
+        paired_chips if whole_fit else on_device,
         mesh=mesh,
         in_specs=(
             P("dp", "ctx", None),

time: 1520 us -> 411 us (0.27)
  blocking collectives: 867 us -> 0 us
  waiting for transfers between devices: 357 us -> 177 us
  starting transfers between devices: 0.94 us -> 127 us
  matrix products: 121 us -> 37.9 us
  local copies, waits for them, and re-layouts: 84.4 us -> 26.2 us
  other arithmetic: 59.8 us -> 24.3 us
    psum x1 -> x0, blocking collectives: 770 us -> none  [on_device(): everywhere = lax.psum(terms, 'ctx')]
    all_gather x12 -> x0, waiting for transfers between devices: 235 us -> none  [the longest x2 68.2 us: one_sequence(): key_piece = lax.all_gather(keys.reshape(rows, D), 'ctx', axis=0, tiled=True)]
    ppermute x0 -> x88, waiting for transfers between devices: none -> 177 us  [the longest x78 177 us: send(): lax.ppermute(values, ('dp', 'ctx'), [(i, i ^ mask) for i in range(32)])]
    ppermute x0 -> x88, starting transfers between devices: none -> 127 us  [the longest x78 115 us: send(): lax.ppermute(values, ('dp', 'ctx'), [(i, i ^ mask) for i in range(32)])]
    reduce_scatter x4 -> x0, waiting for transfers between devices: 118 us -> none  [the longest x1 40.9 us: on_device(): lax.psum_scatter(everywhere[2].astype(jnp.bfloat16), 'dp', scatter_dimens...]
    dot_general x52 -> x21, matrix products: 121 us -> 37.9 us  [the longest x1 4.25 us: paired_chips(): jnp.einsum('thd,shd->hts', g_summed, values, preferred_element_type=f32)]
    all_gather x3 -> x0, blocking collectives: 81.8 us -> none  [the longest x2 61.2 us: one_sequence(): all_rows = lax.all_gather(row_term, 'ctx', axis=0, tiled=True)]
    convert_element_type x21 -> x18, other arithmetic: 26.5 us -> 5.81 us  [the longest x12 4.14 us: plus(): (first.astype(jnp.float32) + second.astype(jnp.float32)).astype(jnp.bfloa...]
  transfers between devices with their start and end apart: 16 -> 88, of which waited for: 13 -> 41; matrix products, arithmetic and copies ran while one was open for 12% -> 17% of each run, Pallas kernels for 0% -> 1%
where the time goes in v1:
time: 411 us; the launch traced here: 403 us
  waiting for transfers between devices  177 us (43%)
  starting transfers between devices  127 us (31%)
  matrix products  37.9 us (9%)
  local copies, waits for them, and re-layouts  26.2 us (6%)
  other arithmetic  24.3 us (6%)
  Pallas kernels  7.15 us (2%)
    ppermute x78, waiting for transfers between devices, send(): lax.ppermute(values, ('dp', 'ctx'), [(i, i ^ mask) for i in range(32)])  177 us
    ppermute x78, starting transfers between devices, send(): lax.ppermute(values, ('dp', 'ctx'), [(i, i ^ mask) for i in range(32)])  115 us
    ppermute x10, starting transfers between devices, send_swapped(): lax.ppermute(values, ('dp', 'ctx'), [(i, target(i) ^ mask) for i in range...  12.4 us
  transfers between devices with their start and end apart: 88, of which 41 were waited for; matrix products, arithmetic and copies ran while one was open for 17% of the time, Pallas kernels for 1%

profile of v1, /device:TPU:0, one launch (start us, length us, event | category | flops | bytes accessed | tf_op | source)
XLA Modules:
  0.0 402.8 jit_solution(7840591048089838459)
XLA Ops:
  24.7 4.5 %collective-permute-start.10 = (bf16[192,1152]{1,0:T(8,128)(2,1)}, bf16[192,1152]{1,0:T(8,128)(2,1)}, u32[]{:S(2)}, u32[]{:S(2)}) collective-permute-start(bf16[192,1152]{1,0:T(8,128)(2,1)} %pad_maximum_fusion.14), channel_id=1, source_target_pairs={{0,24},{1,25},{2,26},{3,27},{4,28},{5,29},{6,30},{7,31},{8,16},{9,... | collective-permute-start | bytes 1327112 | tf_op jit(solution)/shard_map/ppermute | solution.py:263
  34.2 4.0 collective-permute-start.15
  42.4 4.1 %collective-permute-start.17 = (bf16[192,768]{1,0:T(8,128)(2,1)}, bf16[192,768]{1,0:T(8,128)(2,1)S(1)}, u32[]{:S(2)}, u32[]{:S(2)}) collective-permute-start(bf16[192,768]{1,0:T(8,128)(2,1)} %get-tuple-element.36), channel_id=1, source_target_pairs={{0,8},{1,9},{2,10},{3,11},{4,12},{5,13},{6,14},{7,15},{8,0},{9,1},... | collective-permute-start | bytes 884744 | tf_op jit(solution)/shard_map/ppermute | solution.py:263
  48.0 8.0 %collective-permute-start.19 = (bf16[192,768]{1,0:T(8,128)(2,1)}, bf16[192,768]{1,0:T(8,128)(2,1)S(1)}, u32[]{:S(2)}, u32[]{:S(2)}) collective-permute-start(bf16[192,768]{1,0:T(8,128)(2,1)} %get-tuple-element.36), channel_id=1, source_target_pairs={{0,24},{1,25},{2,26},{3,27},{4,28},{5,29},{6,30},{7,31},{8,16},{9,... | collective-permute-start | bytes 884744 | tf_op jit(solution)/shard_map/ppermute | solution.py:263
  57.4 5.3 %collective-permute-start.23 = (bf16[192,1152]{1,0:T(8,128)(2,1)}, bf16[192,1152]{1,0:T(8,128)(2,1)S(1)}, u32[]{:S(2)}, u32[]{:S(2)}) collective-permute-start(bf16[192,1152]{1,0:T(8,128)(2,1)} %get-tuple-element.30), channel_id=1, source_target_pairs={{0,8},{1,9},{2,10},{3,11},{4,12},{5,13},{6,14},{7,15},{8,0},{9,1},... | collective-permute-start | bytes 1327112 | tf_op jit(solution)/shard_map/ppermute | solution.py:263
  63.4 5.8 %collective-permute-done.19 = bf16[192,768]{1,0:T(8,128)(2,1)S(1)} collective-permute-done((bf16[192,768]{1,0:T(8,128)(2,1)}, bf16[192,768]{1,0:T(8,128)(2,1)S(1)}, u32[]{:S(2)}, u32[]{:S(2)}) %collective-permute-start.19) | collective-permute-done | bytes 294944 | tf_op jit(solution)/shard_map/ppermute | solution.py:263
  72.5 11.1 %collective-permute-done.9 = bf16[192,1152]{1,0:T(8,128)(2,1)S(1)} collective-permute-done((bf16[192,1152]{1,0:T(8,128)(2,1)S(1)}, bf16[192,1152]{1,0:T(8,128)(2,1)S(1)}, u32[]{:S(2)}, u32[]{:S(2)}) %collective-permute-start.9) | collective-permute-done | bytes 442400 | tf_op jit(solution)/shard_map/ppermute | solution.py:263
  90.9 6.7 %collective-permute-done.25 = bf16[192,1152]{1,0:T(8,128)(2,1)S(1)} collective-permute-done((bf16[192,1152]{1,0:T(8,128)(2,1)S(1)}, bf16[192,1152]{1,0:T(8,128)(2,1)S(1)}, u32[]{:S(2)}, u32[]{:S(2)}) %collective-permute-start.25) | collective-permute-done | bytes 442400 | tf_op jit(solution)/shard_map/ppermute | solution.py:263
  100.5 11.6 %collective-permute-done.21 = bf16[192,2304]{1,0:T(8,128)(2,1)S(1)} collective-permute-done((bf16[192,2304]{1,0:T(8,128)(2,1)S(1)}, bf16[192,2304]{1,0:T(8,128)(2,1)S(1)}, u32[]{:S(2)}, u32[]{:S(2)}) %collective-permute-start.21) | collective-permute-done | bytes 884768 | tf_op jit(solution)/shard_map/ppermute | solution.py:263
  117.8 4.0 fusion
  124.9 4.4 %collective-permute-start.16 = (bf16[256,384]{0,1:T(8,128)(2,1)S(1)}, bf16[256,384]{0,1:T(8,128)(2,1)S(1)}, u32[]{:S(2)}, u32[]{:S(2)}) collective-permute-start(bf16[256,384]{0,1:T(8,128)(2,1)S(1)} %bitcast.269), channel_id=1, source_target_pairs={{0,8},{1,9},{2,10},{3,11},{4,12},{5,13},{6,14},{7,15},{8,0},{9,1},... | collective-permute-start | bytes 589832 | tf_op jit(solution)/shard_map/ppermute | solution.py:263
  129.4 3.9 collective-permute-done.22
  139.2 4.2 %fusion.33.refs_1_ = f32[768,2304]{1,0:T(8,128)} fusion(bf16[256,1152]{1,0:T(8,128)(2,1)S(1)} %get-tuple-element.44, bf16[256,1152]{1,0:T(8,128)(2,1)S(1)} %get-tuple-element.43, f32[256,768]{1,0:T(8,128)S(1)} %get-tuple-element.129, f32[768]{0:T(1024)S(1)} %mul.404, f32[256]{0:T(256)S(1)} %add_rsqrt_fusion.1, f32[256]{0:T(256)S(1)} %broadcast_multiply_fusion.10), kind=kOutput, calls=%fused_computation.88 | convolution fusion | flops 909115392 | bytes 9049088 | tf_op jit(solution)/shard_map/ti,tj->ij/dot_general | solution.py:460
  160.7 4.2 %convolution_convert_fusion = bf16[6,64,1024]{2,1,0:T(8,128)(2,1)S(1)} fusion(bf16[6,512,1024]{2,1,0:T(8,128)(2,1)} %copy-done.4, f32[512,6]{0,1:T(8,128)} %bitcast.275, bf16[256,6,64]{0,2,1:T(8,128)(2,1)} %bitcast.248, bf16[256,6,64]{0,2,1:T(8,128)(2,1)S(1)} %bitcast.245), kind=kOutput, calls=%fused_computation.34 | convolution fusion | flops 404226048 | bytes 7483392 | tf_op jit(solution)/shard_map/hts,thd->shd/dot_general | solution.py:477
  165.2 4.3 %multiply_convert_fusion = bf16[6,512,1024]{2,1,0:T(8,128)(2,1)S(1)} fusion(bf16[6,512,1024]{2,1,0:T(8,128)(2,1)} %copy-done.4, f32[6,512]{1,0:T(8,128)S(1)} %bitcast_divide_fusion, bf16[1024,6,64]{0,2,1:T(8,128)(2,1)S(1)} %bitcast.237, f32[512,6]{0,1:T(8,128)S(1)} %bitcast.276, bf16[256,6,64]{0,2,1:T(8,128)(2,1)S(1)} %bitcast.250, ...), kind=kOutput, calls=%fused_computation | convolution fusion | flops 416415744 | bytes 13787136 | tf_op jit(solution)/shard_map/thd,shd->hts/dot_general | solution.py:473
  175.5 3.9 multiply_reduce_fusion
  197.9 15.9 %collective-permute-done.54 = bf16[8,24,768]{2,1,0:T(8,128)(2,1)S(1)} collective-permute-done((bf16[8,24,768]{2,1,0:T(8,128)(2,1)S(1)}, bf16[8,24,768]{2,1,0:T(8,128)(2,1)S(1)}, u32[]{:S(2)}, u32[]{:S(2)}) %collective-permute-start.54) | collective-permute-done | bytes 294944 | tf_op jit(solution)/shard_map/ppermute | solution.py:263
  237.1 9.2 %collective-permute-done.62 = bf16[4,24,768]{2,1,0:T(8,128)(2,1)S(1)} collective-permute-done((bf16[4,24,768]{2,1,0:T(8,128)(2,1)S(1)}, bf16[4,24,768]{2,1,0:T(8,128)(2,1)S(1)}, u32[]{:S(2)}, u32[]{:S(2)}) %collective-permute-start.62) | collective-permute-done | bytes 147488 | tf_op jit(solution)/shard_map/ppermute | solution.py:263
  257.9 4.6 %collective-permute-start.37 = (bf16[24,1152]{1,0:T(8,128)(2,1)S(1)}, bf16[24,1152]{1,0:T(8,128)(2,1)S(1)}, u32[]{:S(2)}, u32[]{:S(2)}) collective-permute-start(bf16[24,1152]{1,0:T(8,128)(2,1)S(1)} %get-tuple-element.102), channel_id=1, source_target_pairs={{0,2},{1,3},{2,0},{3,1},{4,6},{5,7},{6,4},{7,5},{8,10},{9,11},{10,... | collective-permute-start | bytes 165896 | tf_op jit(solution)/shard_map/ppermute | solution.py:263
  270.5 9.0 %collective-permute-done.32 = bf16[256,768]{1,0:T(8,128)(2,1)S(1)} collective-permute-done((bf16[256,768]{1,0:T(8,128)(2,1)S(1)}, bf16[256,768]{1,0:T(8,128)(2,1)S(1)}, u32[]{:S(2)}, u32[]{:S(2)}) %collective-permute-start.32) | collective-permute-done | bytes 393248 | tf_op jit(solution)/shard_map/ppermute | solution.py:263
  283.8 6.6 %collective-permute-done.49 = bf16[24,1152]{1,0:T(8,128)(2,1)S(1)} collective-permute-done((bf16[24,1152]{1,0:T(8,128)(2,1)S(1)}, bf16[24,1152]{1,0:T(8,128)(2,1)S(1)}, u32[]{:S(2)}, u32[]{:S(2)}) %collective-permute-start.49) | collective-permute-done | bytes 55328 | tf_op jit(solution)/shard_map/ppermute | solution.py:263
  291.5 4.9 %collective-permute-done.50 = bf16[24,1152]{1,0:T(8,128)(2,1)S(1)} collective-permute-done((bf16[24,1152]{1,0:T(8,128)(2,1)S(1)}, bf16[24,1152]{1,0:T(8,128)(2,1)S(1)}, u32[]{:S(2)}, u32[]{:S(2)}) %collective-permute-start.50) | collective-permute-done | bytes 55328 | tf_op jit(solution)/shard_map/ppermute | solution.py:263
  296.4 4.1 %collective-permute-done.40 = bf16[24,1152]{1,0:T(8,128)(2,1)S(1)} collective-permute-done((bf16[24,1152]{1,0:T(8,128)(2,1)S(1)}, bf16[24,1152]{1,0:T(8,128)(2,1)S(1)}, u32[]{:S(2)}, u32[]{:S(2)}) %collective-permute-start.40) | collective-permute-done | bytes 55328 | tf_op jit(solution)/shard_map/ppermute | solution.py:263
  300.6 5.1 %collective-permute-done.41 = bf16[24,1152]{1,0:T(8,128)(2,1)S(1)} collective-permute-done((bf16[24,1152]{1,0:T(8,128)(2,1)S(1)}, bf16[24,1152]{1,0:T(8,128)(2,1)S(1)}, u32[]{:S(2)}, u32[]{:S(2)}) %collective-permute-start.41) | collective-permute-done | bytes 55328 | tf_op jit(solution)/shard_map/ppermute | solution.py:263
  307.2 4.4 %collective-permute-done.42 = bf16[24,1152]{1,0:T(8,128)(2,1)S(1)} collective-permute-done((bf16[24,1152]{1,0:T(8,128)(2,1)S(1)}, bf16[24,1152]{1,0:T(8,128)(2,1)S(1)}, u32[]{:S(2)}, u32[]{:S(2)}) %collective-permute-start.42) | collective-permute-done | bytes 55328 | tf_op jit(solution)/shard_map/ppermute | solution.py:263
  315.1 7.5 %collective-permute-start.78 = (bf16[24,1152]{1,0:T(8,128)(2,1)S(1)}, bf16[24,1152]{1,0:T(8,128)(2,1)S(1)}, u32[]{:S(2)}, u32[]{:S(2)}) collective-permute-start(bf16[24,1152]{1,0:T(8,128)(2,1)S(1)} %get-tuple-element.97), channel_id=1, source_target_pairs={{0,6},{1,7},{2,4},{3,5},{4,2},{5,3},{6,0},{7,1},{8,14},{9,15},{10,... | collective-permute-start | bytes 165896 | tf_op jit(solution)/shard_map/ppermute | solution.py:263
  338.8 4.2 %collective-permute-done.82 = bf16[4,24,1152]{2,1,0:T(8,128)(2,1)S(1)} collective-permute-done((bf16[4,24,1152]{2,1,0:T(8,128)(2,1)S(1)}, bf16[4,24,1152]{2,1,0:T(8,128)(2,1)S(1)}, u32[]{:S(2)}, u32[]{:S(2)}) %collective-permute-start.82) | collective-permute-done | bytes 221216 | tf_op jit(solution)/shard_map/ppermute | solution.py:263
  344.2 13.9 %collective-permute-done.64 = bf16[8,24,2304]{2,1,0:T(8,128)(2,1)S(1)} collective-permute-done((bf16[8,24,2304]{2,1,0:T(8,128)(2,1)S(1)}, bf16[8,24,2304]{2,1,0:T(8,128)(2,1)S(1)}, u32[]{:S(2)}, u32[]{:S(2)}) %collective-permute-start.64) | collective-permute-done | bytes 884768 | tf_op jit(solution)/shard_map/ppermute | solution.py:263
  359.9 8.6 %collective-permute-done.65 = bf16[4,24,2304]{2,1,0:T(8,128)(2,1)S(1)} collective-permute-done((bf16[4,24,2304]{2,1,0:T(8,128)(2,1)S(1)}, bf16[4,24,2304]{2,1,0:T(8,128)(2,1)S(1)}, u32[]{:S(2)}, u32[]{:S(2)}) %collective-permute-start.65) | collective-permute-done | bytes 442400 | tf_op jit(solution)/shard_map/ppermute | solution.py:263
  375.4 4.7 %collective-permute-done.67 = bf16[24,2304]{1,0:T(8,128)(2,1)S(1)} collective-permute-done((bf16[24,2304]{1,0:T(8,128)(2,1)S(1)}, bf16[24,2304]{1,0:T(8,128)(2,1)S(1)}, u32[]{:S(2)}, u32[]{:S(2)}) %collective-permute-start.67) | collective-permute-done | bytes 110624 | tf_op jit(solution)/shard_map/ppermute | solution.py:263
  380.3 4.3 %collective-permute-start.69 = (bf16[24,2304]{1,0:T(8,128)(2,1)S(1)}, bf16[24,2304]{1,0:T(8,128)(2,1)S(1)}, u32[]{:S(2)}, u32[]{:S(2)}) collective-permute-start(bf16[24,2304]{1,0:T(8,128)(2,1)S(1)} %get-tuple-element.18), channel_id=1, source_target_pairs={{0,2},{1,3},{2,0},{3,1},{4,6},{5,7},{6,4},{7,5},{8,10},{9,11},{10,... | collective-permute-start | bytes 331784 | tf_op jit(solution)/shard_map/ppermute | solution.py:263
  391.8 9.2 %collective-permute-done.72 = bf16[4,24,2304]{2,1,0:T(8,128)(2,1)S(1)} collective-permute-done((bf16[4,24,2304]{2,1,0:T(8,128)(2,1)S(1)}, bf16[4,24,2304]{2,1,0:T(8,128)(2,1)S(1)}, u32[]{:S(2)}, u32[]{:S(2)}) %collective-permute-start.72) | collective-permute-done | bytes 442400 | tf_op jit(solution)/shard_map/ppermute | solution.py:263
  (452 shorter events, 194.0 us)
Async XLA Ops:
  2.1 27.8 %collective-permute-start.6 = (bf16[1,2,192]{2,1,0:T(2,128)(2,1)S(1)}, bf16[1,2,192]{2,1,0:T(2,128)(2,1)S(1)}, u32[]{:S(2)}, u32[]{:S(2)}) collective-permute-start(bf16[1,2,192]{2,1,0:T(2,128)(2,1)S(1)} %get-tuple-element.34), channel_id=1, source_target_pairs={{0,16},{1,17},{2,18},{3,19},{4,20},{5,21},{6,22},{7,23},{8,24},{9,... | collective-permute-start | bytes 2312 | tf_op jit(solution)/shard_map/ppermute | solution.py:263
  5.2 24.2 %collective-permute-start.5 = (bf16[1,2,192]{2,1,0:T(2,128)(2,1)S(1)}, bf16[1,2,192]{2,1,0:T(2,128)(2,1)S(1)}, u32[]{:S(2)}, u32[]{:S(2)}) collective-permute-start(bf16[1,2,192]{2,1,0:T(2,128)(2,1)S(1)} %get-tuple-element.34), channel_id=1, source_target_pairs={{0,8},{1,9},{2,10},{3,11},{4,12},{5,13},{6,14},{7,15},{8,0},{9,1},... | collective-permute-start | bytes 2312 | tf_op jit(solution)/shard_map/ppermute | solution.py:263
  5.2 26.3 %collective-permute-start.7 = (bf16[1,2,192]{2,1,0:T(2,128)(2,1)S(1)}, bf16[1,2,192]{2,1,0:T(2,128)(2,1)S(1)}, u32[]{:S(2)}, u32[]{:S(2)}) collective-permute-start(bf16[1,2,192]{2,1,0:T(2,128)(2,1)S(1)} %get-tuple-element.34), channel_id=1, source_target_pairs={{0,24},{1,25},{2,26},{3,27},{4,28},{5,29},{6,30},{7,31},{8,16},{9,... | collective-permute-start | bytes 2312 | tf_op jit(solution)/shard_map/ppermute | solution.py:263
  6.1 23.1 %collective-permute-start.12 = (s32[128]{0:T(128)S(1)}, s32[128]{0:T(128)S(1)}, u32[]{:S(2)}, u32[]{:S(2)}) collective-permute-start(s32[128]{0:T(128)S(1)} %get-tuple-element.120), channel_id=1, source_target_pairs={{0,2},{1,3},{2,0},{3,1},{4,10},{5,11},{6,8},{7,9},{8,6},{9,7},{10,... | collective-permute-start | bytes 1544 | tf_op jit(solution)/shard_map/ppermute | solution.py:271
  8.1 16.6 %collective-permute-start.11 = (s32[128]{0:T(128)S(1)}, s32[128]{0:T(128)S(1)}, u32[]{:S(2)}, u32[]{:S(2)}) collective-permute-start(s32[128]{0:T(128)S(1)} %get-tuple-element.121), channel_id=1, source_target_pairs={{0,0},{1,1},{2,2},{3,3},{4,8},{5,9},{6,10},{7,11},{8,4},{9,5},{10,... | collective-permute-start | bytes 1544 | tf_op jit(solution)/shard_map/ppermute | solution.py:271
  24.7 60.5 %collective-permute-start.10 = (bf16[192,1152]{1,0:T(8,128)(2,1)}, bf16[192,1152]{1,0:T(8,128)(2,1)}, u32[]{:S(2)}, u32[]{:S(2)}) collective-permute-start(bf16[192,1152]{1,0:T(8,128)(2,1)} %pad_maximum_fusion.14), channel_id=1, source_target_pairs={{0,24},{1,25},{2,26},{3,27},{4,28},{5,29},{6,30},{7,31},{8,16},{9,... | collective-permute-start | bytes 1327112 | tf_op jit(solution)/shard_map/ppermute | solution.py:263
  29.2 42.1 %collective-permute-start.8 = (bf16[192,1152]{1,0:T(8,128)(2,1)}, bf16[192,1152]{1,0:T(8,128)(2,1)}, u32[]{:S(2)}, u32[]{:S(2)}) collective-permute-start(bf16[192,1152]{1,0:T(8,128)(2,1)} %pad_maximum_fusion.14), channel_id=1, source_target_pairs={{0,8},{1,9},{2,10},{3,11},{4,12},{5,13},{6,14},{7,15},{8,0},{9,1},... | collective-permute-start | bytes 1327112 | tf_op jit(solution)/shard_map/ppermute | solution.py:263
  42.4 13.7 %collective-permute-start.17 = (bf16[192,768]{1,0:T(8,128)(2,1)}, bf16[192,768]{1,0:T(8,128)(2,1)S(1)}, u32[]{:S(2)}, u32[]{:S(2)}) collective-permute-start(bf16[192,768]{1,0:T(8,128)(2,1)} %get-tuple-element.36), channel_id=1, source_target_pairs={{0,8},{1,9},{2,10},{3,11},{4,12},{5,13},{6,14},{7,15},{8,0},{9,1},... | collective-permute-start | bytes 884744 | tf_op jit(solution)/shard_map/ppermute | solution.py:263
  48.0 21.2 %collective-permute-start.19 = (bf16[192,768]{1,0:T(8,128)(2,1)}, bf16[192,768]{1,0:T(8,128)(2,1)S(1)}, u32[]{:S(2)}, u32[]{:S(2)}) collective-permute-start(bf16[192,768]{1,0:T(8,128)(2,1)} %get-tuple-element.36), channel_id=1, source_target_pairs={{0,24},{1,25},{2,26},{3,27},{4,28},{5,29},{6,30},{7,31},{8,16},{9,... | collective-permute-start | bytes 884744 | tf_op jit(solution)/shard_map/ppermute | solution.py:263
  56.1 34.7 %collective-permute-start.24 = (bf16[192,1152]{1,0:T(8,128)(2,1)}, bf16[192,1152]{1,0:T(8,128)(2,1)S(1)}, u32[]{:S(2)}, u32[]{:S(2)}) collective-permute-start(bf16[192,1152]{1,0:T(8,128)(2,1)} %get-tuple-element.30), channel_id=1, source_target_pairs={{0,16},{1,17},{2,18},{3,19},{4,20},{5,21},{6,22},{7,23},{8,24},{9,... | collective-permute-start | bytes 1327112 | tf_op jit(solution)/shard_map/ppermute | solution.py:263
  57.4 31.8 %collective-permute-start.23 = (bf16[192,1152]{1,0:T(8,128)(2,1)}, bf16[192,1152]{1,0:T(8,128)(2,1)S(1)}, u32[]{:S(2)}, u32[]{:S(2)}) collective-permute-start(bf16[192,1152]{1,0:T(8,128)(2,1)} %get-tuple-element.30), channel_id=1, source_target_pairs={{0,8},{1,9},{2,10},{3,11},{4,12},{5,13},{6,14},{7,15},{8,0},{9,1},... | collective-permute-start | bytes 1327112 | tf_op jit(solution)/shard_map/ppermute | solution.py:263
  69.2 14.4 %collective-permute-start.9 = (bf16[192,1152]{1,0:T(8,128)(2,1)S(1)}, bf16[192,1152]{1,0:T(8,128)(2,1)S(1)}, u32[]{:S(2)}, u32[]{:S(2)}) collective-permute-start(bf16[192,1152]{1,0:T(8,128)(2,1)S(1)} %copy-done.35), channel_id=1, source_target_pairs={{0,16},{1,17},{2,18},{3,19},{4,20},{5,21},{6,22},{7,23},{8,24},{9,... | collective-permute-start | bytes 1327112 | tf_op jit(solution)/shard_map/ppermute | solution.py:263
  71.4 26.3 %collective-permute-start.25 = (bf16[192,1152]{1,0:T(8,128)(2,1)S(1)}, bf16[192,1152]{1,0:T(8,128)(2,1)S(1)}, u32[]{:S(2)}, u32[]{:S(2)}) collective-permute-start(bf16[192,1152]{1,0:T(8,128)(2,1)S(1)} %copy-done.37), channel_id=1, source_target_pairs={{0,24},{1,25},{2,26},{3,27},{4,28},{5,29},{6,30},{7,31},{8,16},{9,... | collective-permute-start | bytes 1327112 | tf_op jit(solution)/shard_map/ppermute | solution.py:263
  83.6 28.4 %collective-permute-start.21 = (bf16[192,2304]{1,0:T(8,128)(2,1)S(1)}, bf16[192,2304]{1,0:T(8,128)(2,1)S(1)}, u32[]{:S(2)}, u32[]{:S(2)}) collective-permute-start(bf16[192,2304]{1,0:T(8,128)(2,1)S(1)} %copy-done.28), channel_id=1, source_target_pairs={{0,16},{1,17},{2,18},{3,19},{4,20},{5,21},{6,22},{7,23},{8,24},{9,... | collective-permute-start | bytes 2654216 | tf_op jit(solution)/shard_map/ppermute | solution.py:263
  85.3 15.1 %collective-permute-start.20 = (bf16[192,2304]{1,0:T(8,128)(2,1)S(1)}, bf16[192,2304]{1,0:T(8,128)(2,1)S(1)}, u32[]{:S(2)}, u32[]{:S(2)}) collective-permute-start(bf16[192,2304]{1,0:T(8,128)(2,1)S(1)} %copy-done.28), channel_id=1, source_target_pairs={{0,8},{1,9},{2,10},{3,11},{4,12},{5,13},{6,14},{7,15},{8,0},{9,1},... | collective-permute-start | bytes 2654216 | tf_op jit(solution)/shard_map/ppermute | solution.py:263
  97.6 35.6 %collective-permute-start.22 = (bf16[192,2304]{1,0:T(8,128)(2,1)S(1)}, bf16[192,2304]{1,0:T(8,128)(2,1)S(1)}, u32[]{:S(2)}, u32[]{:S(2)}) collective-permute-start(bf16[192,2304]{1,0:T(8,128)(2,1)S(1)} %copy-done.28), channel_id=1, source_target_pairs={{0,24},{1,25},{2,26},{3,27},{4,28},{5,29},{6,30},{7,31},{8,16},{9,... | collective-permute-start | bytes 2654216 | tf_op jit(solution)/shard_map/ppermute | solution.py:263
  145.8 13.2 %collective-permute-start.30 = (bf16[256,384]{1,0:T(8,128)(2,1)}, bf16[256,384]{1,0:T(8,128)(2,1)}, u32[]{:S(2)}, u32[]{:S(2)}) collective-permute-start(bf16[256,384]{1,0:T(8,128)(2,1)} %get-tuple-element.85), channel_id=1, source_target_pairs={{0,8},{1,9},{2,10},{3,11},{4,12},{5,13},{6,14},{7,15},{8,0},{9,1},... | collective-permute-start | bytes 589832 | tf_op jit(solution)/shard_map/ppermute | solution.py:263
  145.8 166.7 %collective-permute-start.26 = (bf16[128,768]{1,0:T(8,128)(2,1)}, bf16[128,768]{1,0:T(8,128)(2,1)}, u32[]{:S(2)}, u32[]{:S(2)}) collective-permute-start(bf16[128,768]{1,0:T(8,128)(2,1)} %get-tuple-element.90), channel_id=1, source_target_pairs={{0,0},{1,1},{2,2},{3,3},{4,8},{5,9},{6,10},{7,11},{8,4},{9,5},{10,... | collective-permute-start | bytes 589832 | tf_op jit(solution)/shard_map/ppermute | solution.py:271
  151.0 41.0 %collective-permute-start.53 = (bf16[2,8,24,768]{3,2,1,0:T(8,128)(2,1)}, bf16[2,8,24,768]{3,2,1,0:T(8,128)(2,1)}, u32[]{:S(2)}, u32[]{:S(2)}) collective-permute-start(bf16[2,8,24,768]{3,2,1,0:T(8,128)(2,1)} %bitcast.51), channel_id=1, source_target_pairs={{0,8},{1,9},{2,10},{3,11},{4,12},{5,13},{6,14},{7,15},{8,0},{9,1},... | collective-permute-start | bytes 1769480 | tf_op jit(solution)/shard_map/ppermute | solution.py:263
  152.6 61.9 %collective-permute-start.73 = (bf16[2,8,24,1152]{3,2,1,0:T(8,128)(2,1)}, bf16[2,8,24,1152]{3,2,1,0:T(8,128)(2,1)}, u32[]{:S(2)}, u32[]{:S(2)}) collective-permute-start(bf16[2,8,24,1152]{3,2,1,0:T(8,128)(2,1)} %bitcast.75), channel_id=1, source_target_pairs={{0,8},{1,9},{2,10},{3,11},{4,12},{5,13},{6,14},{7,15},{8,0},{9,1},... | collective-permute-start | bytes 2654216 | tf_op jit(solution)/shard_map/ppermute | solution.py:263
  186.8 42.5 %collective-permute-start.35 = (bf16[16,24,1152]{2,1,0:T(8,128)(2,1)S(1)}, bf16[16,24,1152]{2,1,0:T(8,128)(2,1)S(1)}, u32[]{:S(2)}, u32[]{:S(2)}) collective-permute-start(bf16[16,24,1152]{2,1,0:T(8,128)(2,1)S(1)} %slice.450), channel_id=1, source_target_pairs={{0,16},{1,17},{2,18},{3,19},{4,20},{5,21},{6,22},{7,23},{8,24},{9,... | collective-permute-start | bytes 2654216 | tf_op jit(solution)/shard_map/ppermute | solution.py:263
  192.1 23.9 %collective-permute-start.31 = (bf16[2,256,768]{2,1,0:T(8,128)(2,1)S(1)}, bf16[2,256,768]{2,1,0:T(8,128)(2,1)S(1)}, u32[]{:S(2)}, u32[]{:S(2)}) collective-permute-start(bf16[2,256,768]{2,1,0:T(8,128)(2,1)S(1)} %slice_bitcast_fusion.2), channel_id=1, source_target_pairs={{0,8},{1,9},{2,10},{3,11},{4,12},{5,13},{6,14},{7,15},{8,0},{9,1},... | collective-permute-start | bytes 2359304 | tf_op jit(solution)/shard_map/ppermute | solution.py:263
  196.7 17.1 %collective-permute-start.54 = (bf16[8,24,768]{2,1,0:T(8,128)(2,1)S(1)}, bf16[8,24,768]{2,1,0:T(8,128)(2,1)S(1)}, u32[]{:S(2)}, u32[]{:S(2)}) collective-permute-start(bf16[8,24,768]{2,1,0:T(8,128)(2,1)S(1)} %slice_bitcast_fusion.8), channel_id=1, source_target_pairs={{0,16},{1,17},{2,18},{3,19},{4,20},{5,21},{6,22},{7,23},{8,24},{9,... | collective-permute-start | bytes 884744 | tf_op jit(solution)/shard_map/ppermute | solution.py:263
  223.5 89.6 %collective-permute-start.27 = (bf16[128,768]{1,0:T(8,128)(2,1)S(1)}, bf16[128,768]{1,0:T(8,128)(2,1)S(1)}, u32[]{:S(2)}, u32[]{:S(2)}) collective-permute-start(bf16[128,768]{1,0:T(8,128)(2,1)S(1)} %copy-done.40), channel_id=1, source_target_pairs={{0,2},{1,3},{2,0},{3,1},{4,10},{5,11},{6,8},{7,9},{8,6},{9,7},{10,... | collective-permute-start | bytes 589832 | tf_op jit(solution)/shard_map/ppermute | solution.py:271
  233.7 14.1 %collective-permute-start.44 = (bf16[4,24,1152]{2,1,0:T(8,128)(2,1)S(1)}, bf16[4,24,1152]{2,1,0:T(8,128)(2,1)S(1)}, u32[]{:S(2)}, u32[]{:S(2)}) collective-permute-start(bf16[4,24,1152]{2,1,0:T(8,128)(2,1)S(1)} %get-tuple-element.69), channel_id=1, source_target_pairs={{0,1},{1,0},{2,3},{3,2},{4,5},{5,4},{6,7},{7,6},{8,9},{9,8},{10,11... | collective-permute-start | bytes 663560 | tf_op jit(solution)/shard_map/ppermute | solution.py:263
  248.5 13.9 %collective-permute-start.47 = (bf16[24,1152]{1,0:T(8,128)(2,1)S(1)}, bf16[24,1152]{1,0:T(8,128)(2,1)S(1)}, u32[]{:S(2)}, u32[]{:S(2)}) collective-permute-start(bf16[24,1152]{1,0:T(8,128)(2,1)S(1)} %get-tuple-element.100), channel_id=1, source_target_pairs={{0,6},{1,7},{2,4},{3,5},{4,2},{5,3},{6,0},{7,1},{8,14},{9,15},{10,... | collective-permute-start | bytes 165896 | tf_op jit(solution)/shard_map/ppermute | solution.py:263
  265.6 72.1 %collective-permute-start.63 = (bf16[2,8,24,2304]{3,2,1,0:T(8,128)(2,1)S(1)}, bf16[2,8,24,2304]{3,2,1,0:T(8,128)(2,1)S(1)}, u32[]{:S(2)}, u32[]{:S(2)}) collective-permute-start(bf16[2,8,24,2304]{3,2,1,0:T(8,128)(2,1)S(1)} %bitcast.239), channel_id=1, source_target_pairs={{0,8},{1,9},{2,10},{3,11},{4,12},{5,13},{6,14},{7,15},{8,0},{9,1},... | collective-permute-start | bytes 5308424 | tf_op jit(solution)/shard_map/ppermute | solution.py:263
  268.9 43.4 %collective-permute-start.75 = (bf16[4,24,1152]{2,1,0:T(8,128)(2,1)S(1)}, bf16[4,24,1152]{2,1,0:T(8,128)(2,1)S(1)}, u32[]{:S(2)}, u32[]{:S(2)}) collective-permute-start(bf16[4,24,1152]{2,1,0:T(8,128)(2,1)S(1)} %slice.494), channel_id=1, source_target_pairs={{0,1},{1,0},{2,3},{3,2},{4,5},{5,4},{6,7},{7,6},{8,9},{9,8},{10,11... | collective-permute-start | bytes 663560 | tf_op jit(solution)/shard_map/ppermute | solution.py:263
  312.5 19.1 %collective-permute-start.43 = (bf16[4,24,1152]{2,1,0:T(8,128)(2,1)S(1)}, bf16[4,24,1152]{2,1,0:T(8,128)(2,1)S(1)}, u32[]{:S(2)}, u32[]{:S(2)}) collective-permute-start(bf16[4,24,1152]{2,1,0:T(8,128)(2,1)S(1)} %pad_maximum_fusion.24), channel_id=1, source_target_pairs={{0,1},{1,0},{2,3},{3,2},{4,5},{5,4},{6,7},{7,6},{8,9},{9,8},{10,11... | collective-permute-start | bytes 663560 | tf_op jit(solution)/shard_map/ppermute | solution.py:263
  313.1 15.8 %collective-permute-start.76 = (bf16[24,1152]{1,0:T(8,128)(2,1)S(1)}, bf16[24,1152]{1,0:T(8,128)(2,1)S(1)}, u32[]{:S(2)}, u32[]{:S(2)}) collective-permute-start(bf16[24,1152]{1,0:T(8,128)(2,1)S(1)} %get-tuple-element.96), channel_id=1, source_target_pairs={{0,2},{1,3},{2,0},{3,1},{4,6},{5,7},{6,4},{7,5},{8,10},{9,11},{10,... | collective-permute-start | bytes 165896 | tf_op jit(solution)/shard_map/ppermute | solution.py:263
  315.1 14.3 %collective-permute-start.78 = (bf16[24,1152]{1,0:T(8,128)(2,1)S(1)}, bf16[24,1152]{1,0:T(8,128)(2,1)S(1)}, u32[]{:S(2)}, u32[]{:S(2)}) collective-permute-start(bf16[24,1152]{1,0:T(8,128)(2,1)S(1)} %get-tuple-element.97), channel_id=1, source_target_pairs={{0,6},{1,7},{2,4},{3,5},{4,2},{5,3},{6,0},{7,1},{8,14},{9,15},{10,... | collective-permute-start | bytes 165896 | tf_op jit(solution)/shard_map/ppermute | solution.py:263
  338.2 19.9 %collective-permute-start.64 = (bf16[8,24,2304]{2,1,0:T(8,128)(2,1)S(1)}, bf16[8,24,2304]{2,1,0:T(8,128)(2,1)S(1)}, u32[]{:S(2)}, u32[]{:S(2)}) collective-permute-start(bf16[8,24,2304]{2,1,0:T(8,128)(2,1)S(1)} %slice_bitcast_fusion), channel_id=1, source_target_pairs={{0,16},{1,17},{2,18},{3,19},{4,20},{5,21},{6,22},{7,23},{8,24},{9,... | collective-permute-start | bytes 2654216 | tf_op jit(solution)/shard_map/ppermute | solution.py:263
  (102 other events, 817.5 us)
